TPU v7x, 256 devices: a whole 4x4x8 slice. The times are simulated.
256 devices in a mesh: dp: 32 (over x, z), ctx: 8 (over y, core).
Axes of the slice: x: 4, y: 4, z: 8, core: 2. Of those that a mesh axis runs over, the one named last changes fastest.
Arguments:
- hidden: bfloat16 [32, 2048, 4096], P('dp', 'ctx'), may hold values from -6 to 6
- segments: int32 [32, 2048], P('dp', 'ctx'), may hold values from 0 to 15, as said below
- gain: float32 [4096], replicated, may hold values from 0.25 to 1.75
- inv_temp: float32 [], replicated, may hold values from 20 to 50
- positives: int32 [512], P(('dp', 'ctx')), may hold values from 0 to 511, as said below
Outputs:
- grad_hidden: bfloat16 [32, 2048, 4096], P('dp', 'ctx')
- grad_gain: float32 [4096], replicated
- loss: float32 [], replicated
Inputs may be any that keep to these rules, and one draw needn't show every extreme that they name: `segments`: in each sequence the document numbers never fall along positions and every document has one position or more; document 0 covers more than half of the sequence's positions. `positives`: no document is its own positive.
All inputs are finite; a program needn't handle non-finite values.
Results may differ from a plain program's by a relative error of at most 0.0053.
Values may be sent and summed in bfloat16 or wider, within the bound.
A program may use at most 64 MiB of HBM per device.

v0:
```python
import jax
import jax.numpy as jnp
from jax import lax
from jax.sharding import PartitionSpec as P

DOCS_DEV = 2


def normalize_docs(pooled_totals, counts):
    pooled = pooled_totals / counts[:, None]
    rnorm = lax.rsqrt(jnp.sum(pooled * pooled, axis=-1, keepdims=True) + 1e-06)
    return (pooled * rnorm, rnorm)


def body(hidden, segments, gain, inv_temp, positives):
    states = hidden[0].astype(jnp.float32)
    scale_t = lax.rsqrt(jnp.mean(states * states, axis=-1, keepdims=True) + 1e-06)
    normalized_rows = states * scale_t * gain
    ctx_count = lax.axis_size("ctx")
    seq_docs = DOCS_DEV * ctx_count
    document_indicator = (
        segments[0][:, None] == jnp.arange(seq_docs, dtype=jnp.int32)[None, :]
    ).astype(jnp.float32)
    pooled_totals = lax.dot_general(
        document_indicator,
        normalized_rows,
        (((0,), (0,)), ((), ())),
        precision=lax.Precision.HIGHEST,
    )
    counts = jnp.sum(document_indicator, axis=0)
    ctx_rank = lax.axis_index("ctx")
    own_sums, own_counts = (
        lax.psum_scatter(pooled_totals, "ctx", scatter_dimension=0, tiled=True),
        lax.psum_scatter(counts, "ctx", scatter_dimension=0, tiled=True),
    )
    emb_f, rnorm = normalize_docs(own_sums, own_counts)
    emb_own = emb_f.astype(jnp.bfloat16)
    emb_all = lax.all_gather(emb_own, ("dp", "ctx"), axis=0, tiled=True)
    all_docs = emb_all.shape[0]
    row_first = (lax.axis_index("dp") * ctx_count + ctx_rank) * DOCS_DEV
    logits = (
        lax.dot_general(
            emb_own, emb_all, (((1,), (1,)), ((), ())), preferred_element_type=jnp.float32
        )
        * inv_temp
    )
    columns = jnp.arange(all_docs, dtype=jnp.int32)[None, :]
    own_rows = row_first + jnp.arange(DOCS_DEV, dtype=jnp.int32)[:, None]
    pos_mask = (columns == positives[:, None]).astype(jnp.float32)
    logits = jnp.where(columns == own_rows, -1e30, logits)
    top = jnp.max(logits, axis=1, keepdims=True)
    expo = jnp.exp(logits - top)
    total = jnp.sum(expo, axis=1, keepdims=True)
    lse = top[:, 0] + jnp.log(total[:, 0])
    loss_local = jnp.sum(lse - jnp.sum(pos_mask * logits, axis=1)) / all_docs
    gmat = ((expo / total - pos_mask) * (inv_temp / all_docs)).astype(jnp.bfloat16)
    row_grad = jnp.dot(gmat, emb_all, preferred_element_type=jnp.float32)
    grad_rows = lax.all_gather(gmat, ("dp", "ctx"), axis=0, tiled=True)
    grad_cols = lax.dynamic_slice_in_dim(grad_rows, row_first, DOCS_DEV, 1)
    col_grad = lax.dot_general(
        grad_cols, emb_all, (((0,), (0,)), ((), ())), preferred_element_type=jnp.float32
    )
    demb = row_grad + col_grad
    dpool = rnorm * (demb - emb_f * jnp.sum(emb_f * demb, axis=-1, keepdims=True))
    dsum_own = dpool / own_counts[:, None]
    dsum_seq = lax.all_gather(dsum_own, "ctx", axis=0, tiled=True)
    normalized_gradient = jnp.dot(document_indicator, dsum_seq, precision=lax.Precision.HIGHEST)
    gain_local = jnp.sum(normalized_gradient * states * scale_t, axis=0)
    grad_gain, loss = lax.psum((gain_local, loss_local), ("dp", "ctx"))
    grad_out = normalized_gradient * gain
    inner = jnp.mean(grad_out * states, axis=-1, keepdims=True)
    grad_hidden = (scale_t * grad_out - states * scale_t**3 * inner).astype(jnp.bfloat16)
    return (grad_hidden[None], grad_gain, loss)


def solution(mesh):
    return jax.shard_map(
        body,
        mesh=mesh,
        in_specs=(P("dp", "ctx", None), P("dp", "ctx"), P(), P(), P(("dp", "ctx"))),
        out_specs=(P("dp", "ctx", None), P(), P()),
        check_vma=False,
    )
```

profile of v0, /device:TPU:1, one launch (start us, length us, event | category | flops | bytes accessed | tf_op | source)
XLA Modules:
  0.0 389.6 jit_solution(4266364074889755771)
XLA Ops:
  7.2 2.1 fusion
  9.3 4.2 %fusion.2 = f32[16,4096]{1,0:T(8,128)} fusion(bf16[1,256,4096]{2,1,0:T(8,128)(2,1)} %param.5, f32[4096]{0:T(1024)} %param.7, f32[256]{0:T(256)S(1)} %get-tuple-element.12, s32[256]{0:T(256)} %bitcast.26), kind=kOutput, calls=%fused_computation.8 | convolution fusion | flops 204476416 | bytes 2377728 | tf_op jit(solution)/shard_map/dot_general | solution.py:24
  13.6 0.6 dynamic-slice
  14.8 0.1 convert_reduce_fusion
  15.0 15.0 %all-reduce.1 = f32[16]{0:T(128)S(1)} all-reduce(f32[16]{0:T(128)S(1)} %convert_reduce_fusion), channel_id=3, replica_groups=mesh['dp'=32,'ctx'=8] {'ctx'}, use_global_device_ids=true, to_apply=%region_3.0.clone | all-reduce | flops 16 | bytes 128
  30.0 50.8 %all-reduce.5.cloned.1.call-done = f32[16,4096]{1,0:T(8,128)} async-done(((f32[16,4096]{1,0:T(8,128)}), f32[16,4096]{1,0:T(8,128)}) %all-reduce.5.cloned.1.call-update) | async-done | bytes 262160
  80.8 1.1 multiply_reduce_fusion.1
  81.9 0.7 fusion.30
  83.3 119.1 %all-gather.5.cloned.1.call-done = bf16[256,2,4096]{2,1,0:T(2,128)(2,1)} async-done(((bf16[1,2,4096]{2,1,0:T(2,128)(2,1)}), bf16[256,2,4096]{2,1,0:T(2,128)(2,1)}) %all-gather.5.cloned.1.call-update) | async-done | bytes 4194320 | tf_op jit(solution)/shard_map/all_gather | solution.py:38
  202.4 7.2 %reshape.46 = bf16[512,4096]{1,0:T(8,128)(2,1)} reshape(bf16[256,2,4096]{2,1,0:T(2,128)(2,1)} %all-gather.5.cloned.1.call-done) | data formatting | bytes 8388608
  209.6 3.6 fusion.21
  213.3 0.2 select_reduce_fusion
  213.5 0.1 fusion.29
  213.6 0.7 fusion.22
  214.3 0.6 subtract_reduce_fusion
  215.6 67.0 %all-gather.1 = bf16[256,2,512]{2,1,0:T(2,128)(2,1)S(1)} all-gather(bf16[1,2,512]{2,1,0:T(2,128)(2,1)S(1)} %fusion.29), channel_id=1, replica_groups=mesh['dp'=32,'ctx'=8] {'dp','ctx'}, dimensions={0}, use_global_device_ids=true | all-gather | bytes 526336 | tf_op jit(solution)/shard_map/all_gather | solution.py:58
  282.6 0.2 reshape.48
  282.8 3.1 multiply_reduce_fusion
  285.9 0.1 divide_bitcast_fusion
  286.0 12.8 %all-gather.2 = f32[8,2,4096]{2,1,0:T(2,128)S(1)} all-gather(f32[1,2,4096]{2,1,0:T(2,128)S(1)} %divide_bitcast_fusion), channel_id=1, replica_groups=mesh['dp'=32,'ctx'=8] {'ctx'}, dimensions={0}, use_global_device_ids=true | all-gather | bytes 294912 | tf_op jit(solution)/shard_map/all_gather | solution.py:66
  298.8 0.2 reshape.50
  299.0 4.8 %fusion.9 = (f32[4096]{0:T(1024)S(1)}, f32[256]{0:T(256)S(1)}, f32[256,4096]{1,0:T(8,128)}) fusion(bf16[1,256,4096]{2,1,0:T(8,128)(2,1)S(1)} %copy-done.1, f32[256]{0:T(256)S(1)} %get-tuple-element.12, f32[4096]{0:T(1024)S(1)} %copy-done.2, f32[16,4096]{1,0:T(8,128)S(1)} %reshape.50, s32[256]{0:T(256)S(1)} %bitcast.28), kind=kOutput, calls=%fused_computation.14 | convolution fusion | flops 208666368 | bytes 6589440 | tf_op jit(solution)/shard_map/dot_general | solution.py:67
  303.8 74.0 %all-reduce.2 = (f32[4096]{0:T(1024)}, f32[]{:T(128)}) all-reduce(f32[4096]{0:T(1024)S(1)} %get-tuple-element.3, f32[]{:T(128)S(6)} %div.42), channel_id=1, replica_groups=mesh['dp'=32,'ctx'=8] {'dp','ctx'}, use_global_device_ids=true, to_apply=%region_10.11 | all-reduce | flops 4097 | bytes 32776 | tf_op jit(solution)/shard_map/psum | solution.py:69
  377.8 5.0 %fusion.10 = bf16[1,256,4096]{2,1,0:T(8,128)(2,1)} fusion(f32[256,4096]{1,0:T(8,128)} %get-tuple-element.17, bf16[1,256,4096]{2,1,0:T(8,128)(2,1)S(1)} %copy-done.1, f32[256]{0:T(256)S(1)} %broadcast_multiply_fusion, f32[256]{0:T(256)S(1)} %get-tuple-element.11, f32[4096]{0:T(1024)S(1)} %copy-done.2, f32[256]{0:T(256)S(1)} %get-tuple-element.12), kind=kLoop, calls=%fused_computation.15 | loop fusion | flops 7340032 | bytes 8408064 | tf_op jit(solution)/shard_map/broadcast_in_dim | solution.py:73
  (21 shorter events, 0.2 us)
Async XLA Ops:
  7.2 6.4 %copy-start.5 = (u32[256]{0:T(256)S(1)}, u32[256]{0:T(256)}, u32[]{:S(2)}) copy-start(u32[256]{0:T(256)} %constant.40) | copy-start | bytes 3076
  7.2 7.7 %copy-start.4 = (s32[1,256]{1,0:T(1,128)S(1)}, s32[1,256]{1,0:T(1,128)}, u32[]{:S(2)}) copy-start(s32[1,256]{1,0:T(1,128)} %param.6) | copy-start | bytes 3076
  7.2 73.6 %all-reduce.5.cloned.1.call-start = ((), (), s32[]{:S(2)}) async-start(), calls=%async_computation.1 | async-start | bytes 524288
  13.5 188.9 %all-gather.5.cloned.1.call-start = ((), (), s32[]{:S(2)}) async-start(), calls=%async_computation | async-start | bytes 4210688 | tf_op jit(solution)/shard_map/all_gather | solution.py:38
  209.6 3.6 copy-start.3
  209.6 4.0 %copy-start = (bf16[512,4096]{1,0:T(8,128)(2,1)S(1)}, bf16[512,4096]{1,0:T(8,128)(2,1)}, u32[]{:S(2)}) copy-start(bf16[512,4096]{1,0:T(8,128)(2,1)} %reshape.46) | copy-start | bytes 12582916
  214.3 84.7 %copy-start.1 = (bf16[1,256,4096]{2,1,0:T(8,128)(2,1)S(1)}, bf16[1,256,4096]{2,1,0:T(8,128)(2,1)}, u32[]{:S(2)}) copy-start(bf16[1,256,4096]{2,1,0:T(8,128)(2,1)} %param.5) | copy-start | bytes 6291460
  214.3 84.7 %copy-start.2 = (f32[4096]{0:T(1024)S(1)}, f32[4096]{0:T(1024)}, u32[]{:S(2)}) copy-start(f32[4096]{0:T(1024)} %param.7) | copy-start | bytes 49156
Sparse Core Ops, SparseCore 0:
  13.7 67.1 all-reduce.4
  85.1 117.3 all-gather.4
where the time goes:
time: 390 us
  waiting for transfers between devices  170 us (44%)
  blocking collectives  169 us (43%)
  matrix products  16.3 us (4%)
  between operations  16.1 us (4%)
  other arithmetic  10 us (3%)
  local copies, waits for them, and re-layouts  8.27 us (2%)
    all_gather x1, waiting for transfers between devices, body(): emb_all = lax.all_gather(emb_own, ('dp', 'ctx'), axis=0, tiled=True)  119 us
    psum x1, blocking collectives, body(): grad_gain, loss = lax.psum((gain_local, loss_local), ('dp', 'ctx'))  74 us
    all_gather x1, blocking collectives, body(): grad_rows = lax.all_gather(gmat, ('dp', 'ctx'), axis=0, tiled=True)  67 us
    unnamed x3, waiting for transfers between devices  50.8 us
    unnamed x1, blocking collectives  15 us
    all_gather x1, blocking collectives, body(): dsum_seq = lax.all_gather(dsum_own, 'ctx', axis=0, tiled=True)  12.8 us
    unnamed x17, local copies, waits for them, and re-layouts  8.27 us
  transfers between devices with their start and end apart: 2, of which 2 were waited for; matrix products, arithmetic and copies ran while one was open for 0% of the time, Pallas kernels for 0%

commit v1 on v0

--- a/solution.py
+++ b/solution.py
@@ -66,7 +66,7 @@
     dsum_seq = lax.all_gather(dsum_own, "ctx", axis=0, tiled=True)
     normalized_gradient = jnp.dot(document_indicator, dsum_seq, precision=lax.Precision.HIGHEST)
     gain_local = jnp.sum(normalized_gradient * states * scale_t, axis=0)
-    grad_gain, loss = lax.psum((gain_local, loss_local), ("dp", "ctx"))
+    grad_gain, loss = lax.psum(lax.psum((gain_local, loss_local), "dp"), "ctx")
     grad_out = normalized_gradient * gain
     inner = jnp.mean(grad_out * states, axis=-1, keepdims=True)
     grad_hidden = (scale_t * grad_out - states * scale_t**3 * inner).astype(jnp.bfloat16)

time: 390 us -> 478 us (1.23)
  blocking collectives: 169 us -> 256 us
    psum x1 -> x2, blocking collectives: 74 us -> 162 us  [body(): grad_gain, loss = lax.psum(lax.psum((gain_local, loss_local), 'dp'), 'ctx')]
where the time goes in v1:
time: 478 us; the launch traced here: 477 us
  blocking collectives  256 us (54%)
  waiting for transfers between devices  170 us (36%)
  matrix products  16.3 us (3%)
  between operations  16.1 us (3%)
  other arithmetic  10 us (2%)
  local copies, waits for them, and re-layouts  8.27 us (2%)
    psum x2, blocking collectives, body(): grad_gain, loss = lax.psum(lax.psum((gain_local, loss_local), 'dp'), 'ctx')  162 us
    all_gather x1, waiting for transfers between devices, body(): emb_all = lax.all_gather(emb_own, ('dp', 'ctx'), axis=0, tiled=True)  119 us
    all_gather x1, blocking collectives, body(): grad_rows = lax.all_gather(gmat, ('dp', 'ctx'), axis=0, tiled=True)  67 us
    unnamed x3, waiting for transfers between devices  50.8 us
    unnamed x1, blocking collectives  15 us
    all_gather x1, blocking collectives, body(): dsum_seq = lax.all_gather(dsum_own, 'ctx', axis=0, tiled=True)  12.8 us
  transfers between devices with their start and end apart: 2, of which 2 were waited for; matrix products, arithmetic and copies ran while one was open for 0% of the time, Pallas kernels for 0%

profile of v1, /device:TPU:1, one launch (start us, length us, event | category | flops | bytes accessed | tf_op | source)
XLA Modules:
  0.0 477.2 jit_solution(16398157103624464069)
XLA Ops:
  7.2 2.1 fusion
  9.3 4.2 fusion.2
  13.6 0.6 dynamic-slice
  14.8 0.1 convert_reduce_fusion
  15.0 15.0 %all-reduce.1 = f32[16]{0:T(128)S(1)} all-reduce(f32[16]{0:T(128)S(1)} %convert_reduce_fusion), channel_id=3, replica_groups=mesh['dp'=32,'ctx'=8] {'ctx'}, use_global_device_ids=true, to_apply=%region_3.0.clone | all-reduce | flops 16 | bytes 128
  30.0 50.8 %all-reduce.6.cloned.1.call-done = f32[16,4096]{1,0:T(8,128)} async-done(((f32[16,4096]{1,0:T(8,128)}), f32[16,4096]{1,0:T(8,128)}) %all-reduce.6.cloned.1.call-update) | async-done | bytes 262160
  80.8 1.1 multiply_reduce_fusion.1
  81.9 0.7 fusion.30
  83.3 119.1 %all-gather.5.cloned.1.call-done = bf16[256,2,4096]{2,1,0:T(2,128)(2,1)} async-done(((bf16[1,2,4096]{2,1,0:T(2,128)(2,1)}), bf16[256,2,4096]{2,1,0:T(2,128)(2,1)}) %all-gather.5.cloned.1.call-update) | async-done | bytes 4194320 | tf_op jit(solution)/shard_map/all_gather | solution.py:38
  202.4 7.2 %reshape.46 = bf16[512,4096]{1,0:T(8,128)(2,1)} reshape(bf16[256,2,4096]{2,1,0:T(2,128)(2,1)} %all-gather.5.cloned.1.call-done) | data formatting | bytes 8388608
  209.6 3.6 fusion.21
  213.3 0.2 select_reduce_fusion
  213.6 0.7 fusion.22
  214.3 0.6 subtract_reduce_fusion
  215.6 67.0 %all-gather.1 = bf16[256,2,512]{2,1,0:T(2,128)(2,1)S(1)} all-gather(bf16[1,2,512]{2,1,0:T(2,128)(2,1)S(1)} %fusion.29), channel_id=1, replica_groups=mesh['dp'=32,'ctx'=8] {'dp','ctx'}, dimensions={0}, use_global_device_ids=true | all-gather | bytes 526336 | tf_op jit(solution)/shard_map/all_gather | solution.py:58
  282.6 0.2 reshape.48
  282.8 3.1 multiply_reduce_fusion
  285.9 0.1 divide_bitcast_fusion
  286.0 12.8 %all-gather.2 = f32[8,2,4096]{2,1,0:T(2,128)S(1)} all-gather(f32[1,2,4096]{2,1,0:T(2,128)S(1)} %divide_bitcast_fusion), channel_id=1, replica_groups=mesh['dp'=32,'ctx'=8] {'ctx'}, dimensions={0}, use_global_device_ids=true | all-gather | bytes 294912 | tf_op jit(solution)/shard_map/all_gather | solution.py:66
  298.8 0.2 reshape.50
  299.0 4.8 fusion.9
  303.8 112.9 %all-reduce.2 = (f32[4096]{0:T(1024)S(1)}, f32[]{:T(128)}) all-reduce(f32[4096]{0:T(1024)S(1)} %get-tuple-element.3, f32[]{:T(128)S(6)} %div.42), channel_id=1, replica_groups=mesh['dp'=32,'ctx'=8] {'dp'}, use_global_device_ids=true, to_apply=%region_10.11 | all-reduce | flops 4097 | bytes 32776 | tf_op jit(solution)/shard_map/psum | solution.py:69
  416.6 48.7 %all-reduce.3 = (f32[4096]{0:T(1024)}, f32[]{:T(128)}) all-reduce(f32[4096]{0:T(1024)S(1)} %get-tuple-element.7, f32[]{:T(128)} %get-tuple-element.8), channel_id=1, replica_groups=mesh['dp'=32,'ctx'=8] {'ctx'}, use_global_device_ids=true, to_apply=%region_11.12 | all-reduce | flops 4097 | bytes 32776 | tf_op jit(solution)/shard_map/psum | solution.py:69
  465.4 5.0 %fusion.10 = bf16[1,256,4096]{2,1,0:T(8,128)(2,1)} fusion(f32[256,4096]{1,0:T(8,128)} %get-tuple-element.19, bf16[1,256,4096]{2,1,0:T(8,128)(2,1)S(1)} %copy-done.1, f32[256]{0:T(256)S(1)} %broadcast_multiply_fusion, f32[256]{0:T(256)S(1)} %get-tuple-element.13, f32[4096]{0:T(1024)S(1)} %copy-done.2, f32[256]{0:T(256)S(1)} %get-tuple-element.14), kind=kLoop, calls=%fused_computation.15 | loop fusion | flops 7340032 | bytes 8408064 | tf_op jit(solution)/shard_map/broadcast_in_dim | solution.py:73
  (22 shorter events, 0.3 us)
Async XLA Ops:
  7.2 6.4 %copy-start.5 = (u32[256]{0:T(256)S(1)}, u32[256]{0:T(256)}, u32[]{:S(2)}) copy-start(u32[256]{0:T(256)} %constant.40) | copy-start | bytes 3076
  7.2 7.7 %copy-start.4 = (s32[1,256]{1,0:T(1,128)S(1)}, s32[1,256]{1,0:T(1,128)}, u32[]{:S(2)}) copy-start(s32[1,256]{1,0:T(1,128)} %param.6) | copy-start | bytes 3076
  7.2 73.6 %all-reduce.6.cloned.1.call-start = ((), (), s32[]{:S(2)}) async-start(), calls=%async_computation.1 | async-start | bytes 524288
  13.5 188.9 %all-gather.5.cloned.1.call-start = ((), (), s32[]{:S(2)}) async-start(), calls=%async_computation | async-start | bytes 4210688 | tf_op jit(solution)/shard_map/all_gather | solution.py:38
  209.6 3.6 copy-start.3
  209.6 4.0 copy-start
  214.3 84.7 %copy-start.1 = (bf16[1,256,4096]{2,1,0:T(8,128)(2,1)S(1)}, bf16[1,256,4096]{2,1,0:T(8,128)(2,1)}, u32[]{:S(2)}) copy-start(bf16[1,256,4096]{2,1,0:T(8,128)(2,1)} %param.5) | copy-start | bytes 6291460
  214.3 84.7 %copy-start.2 = (f32[4096]{0:T(1024)S(1)}, f32[4096]{0:T(1024)}, u32[]{:S(2)}) copy-start(f32[4096]{0:T(1024)} %param.7) | copy-start | bytes 49156
Sparse Core Ops, SparseCore 0:
  13.7 67.1 all-reduce.5
  85.1 117.3 all-gather.4
